TPU v7x, 128 devices: a whole 4x4x4 slice. The times are simulated.
128 devices in a mesh: dp: 4 (over z), fsdp: 32 (over y, x, core).
Axes of the slice: x: 4, y: 4, z: 4, core: 2. Of those that a mesh axis runs over, the one named last changes fastest.
Arguments:
- logged: bfloat16 [2048, 8192], P('dp', 'fsdp'), may hold values from -6 to 6
- pairs: int32 [512, 2], P('dp'), may hold values from 0 to 511
- clicks: int32 [512], P('dp'), may hold values 0 or 1
- query_pairs: int32 [32, 2], P('dp'), may hold values from 0 to 511
- query_clicks: int32 [32], P('dp'), may hold values 0 or 1
- first_weight: bfloat16 [8192, 8192], P(None, 'fsdp'), may hold values from -0.0625 to 0.0625
- second_weight: bfloat16 [8192, 8192], P(None, 'fsdp'), may hold values from -0.0625 to 0.0625
- head_weight: float32 [8192], P('fsdp'), may hold values from -0.0625 to 0.0625
Outputs:
- solution: float32 [8192, 8192], P('dp', 'fsdp')
- influence: float32 [512], P('dp')
Inputs may be any that keep to these rules, and one draw needn't show every extreme that they name: Each block of 128 pairs indexes rows within the matching block of 512 logged rows. `query_pairs`: each block of 8 query pairs indexes rows within the matching block of 512 logged rows.
All inputs are finite; a program needn't handle non-finite values. No bound on the sum of `clicks` or of `query_clicks` on one device may be relied on, other than what follows from the above.
Results may differ from a plain program's by a relative error of at most 0.035.
Values may be sent and summed in bfloat16 or wider, within the bound.
A program may use at most 128 MiB of HBM per device.

v0:
```python
import jax
import jax.numpy as jnp
from jax import lax
from jax.sharding import PartitionSpec as P

DAMPING = 0.01


def pair_terms(first_score, second_score, outcome):
    signed = 2.0 * outcome.astype(jnp.float32) - 1.0
    margin = first_score - second_score
    slope_term = -signed * jax.nn.sigmoid(-signed * margin)
    curve_term = jax.nn.sigmoid(signed * margin) * jax.nn.sigmoid(-signed * margin)
    return (slope_term, curve_term)


def solver_total(value):
    return lax.psum(value, ("dp", "fsdp"))


def contract_rows(left, right):
    return lax.dot_general(
        left, right, (((0,), (0,)), ((), ())), preferred_element_type=jnp.float32
    )


def local(
    logged, pairs, clicks, query_pairs, query_clicks, first_weight, second_weight, head_weight
):
    npairs = pairs.shape[0]
    nqueries = query_pairs.shape[0]
    count = 2 * npairs
    row_ids = jnp.concatenate([pairs[:, 0], pairs[:, 1], query_pairs[:, 0], query_pairs[:, 1]])
    local_rows = jnp.take(logged, row_ids, axis=0)
    feats = lax.all_gather(local_rows, "fsdp", axis=1, tiled=True)
    hidden = jnp.tanh(jnp.dot(feats, first_weight, preferred_element_type=jnp.float32)).astype(
        jnp.bfloat16
    )
    second_pre = jnp.dot(
        lax.all_gather(hidden, "fsdp", axis=1, tiled=True),
        second_weight,
        preferred_element_type=jnp.float32,
    )
    output_act = jnp.tanh(second_pre)
    scores_all = lax.psum(jnp.sum(output_act * head_weight, axis=1), "fsdp")
    coef = (head_weight * (1.0 - output_act * output_act)).astype(jnp.bfloat16)
    back_term = lax.dot_general(
        coef, second_weight, (((1,), (1,)), ((), ())), preferred_element_type=jnp.float32
    )
    back = lax.psum_scatter(
        back_term.astype(jnp.bfloat16), "fsdp", scatter_dimension=1, tiled=True
    ).astype(jnp.float32)
    hidden_float = hidden.astype(jnp.float32)
    mixing = (1.0 - hidden_float * hidden_float) * back
    slope_train, curve_train = pair_terms(scores_all[:npairs], scores_all[npairs:count], clicks)
    slope_query = pair_terms(
        scores_all[count : count + nqueries], scores_all[count + nqueries :], query_clicks
    )[0]
    query_err = jnp.concatenate([slope_query, -slope_query])
    query_rows = (query_err[:, None] * mixing[count:]).astype(jnp.bfloat16)
    grad_local = contract_rows(feats[count:], query_rows)
    gradient = lax.psum_scatter(
        grad_local.astype(jnp.bfloat16), "dp", scatter_dimension=0, tiled=True
    ).astype(jnp.float32)
    train_feats = feats[:count]
    train_mix = mixing[:count]

    def apply_curvature(direction):
        packed = direction.astype(jnp.bfloat16)
        gathered = lax.all_gather(packed, "dp", axis=0, tiled=True)
        project = jnp.dot(train_feats, gathered, preferred_element_type=jnp.float32)
        response = lax.psum(jnp.sum(train_mix * project, axis=1), "fsdp")
        rdiff = response[:npairs] - response[npairs:]
        resp_err = jnp.concatenate([curve_train * rdiff, -curve_train * rdiff])
        resp_rows = (resp_err[:, None] * train_mix).astype(jnp.bfloat16)
        term = contract_rows(train_feats, resp_rows)
        return (packed, gathered, term, rdiff)

    norm_first = solver_total(jnp.sum(gradient * gradient))
    packed_first, gathered_first, local_first, rdiff_first = apply_curvature(gradient)
    product_first = lax.psum_scatter(
        local_first.astype(jnp.bfloat16), "dp", scatter_dimension=0, tiled=True
    ).astype(jnp.float32)
    curv_first = (
        solver_total(jnp.sum(packed_first.astype(jnp.float32) * product_first))
        + DAMPING * norm_first
    )
    alpha_first = norm_first / curv_first
    residual_next = gradient - alpha_first * (product_first + DAMPING * gradient)
    norm_next = solver_total(jnp.sum(residual_next * residual_next))
    direction_next = residual_next + norm_next / norm_first * gradient
    packed_next, gathered_next, local_next, rdiff_next = apply_curvature(direction_next)
    damped_part = DAMPING * jnp.sum(direction_next * direction_next)
    product_next = lax.psum_scatter(
        local_next.astype(jnp.bfloat16), "dp", scatter_dimension=0, tiled=True
    ).astype(jnp.float32)
    inner_part = jnp.sum(packed_next.astype(jnp.float32) * product_next) + damped_part
    curv_next = solver_total(inner_part)
    alpha_next = norm_next / curv_next
    solution = alpha_first * gradient + alpha_next * direction_next
    influence = -slope_train * (alpha_first * rdiff_first + alpha_next * rdiff_next)
    return (solution, influence)


def solution(mesh):
    placed = (
        P("dp", "fsdp"),
        P("dp", None),
        P("dp"),
        P("dp", None),
        P("dp"),
        P(None, "fsdp"),
        P(None, "fsdp"),
        P("fsdp"),
    )
    return jax.shard_map(
        local, mesh=mesh, in_specs=placed, out_specs=(P("dp", "fsdp"), P("dp")), check_vma=False
    )
```

profile of v0, /device:TPU:1, one launch (start us, length us, event | category | flops | bytes accessed | tf_op | source)
XLA Modules:
  0.0 815.9 jit_solution(4647815058639752397)
XLA Ops:
  7.2 0.0 copy-start
  7.2 0.0 all-gather.5.cloned.1.call-start
  7.2 0.8 slice_bitcast_fusion.3
  8.0 0.8 slice_bitcast_fusion.1
  8.7 0.1 fusion.33
  8.8 0.0 copy-done
  8.8 2.0 gather_fusion
  10.8 0.1 compare_and_fusion
  10.9 0.8 broadcast_select_fusion
  11.7 0.0 all-gather.5.cloned.1.call-update
  11.7 0.0 copy-start.6
  11.7 0.0 all-gather.7.cloned.1.call-start
  11.8 53.5 %all-gather.5.cloned.1.call-done = bf16[272,8192]{1,0:T(8,128)(2,1)} async-done(((bf16[272,256]{1,0:T(8,128)(2,1)}), bf16[272,8192]{1,0:T(8,128)(2,1)}) %all-gather.5.cloned.1.call-update) | async-done | bytes 4456464 | tf_op jit(solution)/shard_map/all_gather | solution.py:35
  65.2 5.5 fusion.17
  70.8 0.0 all-gather.7.cloned.1.call-update
  70.8 0.0 reduce-scatter.5.cloned.1.call-start
  70.8 49.4 %all-gather.7.cloned.1.call-done = bf16[272,8192]{1,0:T(8,128)(2,1)} async-done(((bf16[272,256]{1,0:T(8,128)(2,1)}), bf16[272,8192]{1,0:T(8,128)(2,1)}) %all-gather.7.cloned.1.call-update) | async-done | bytes 4456464 | tf_op jit(solution)/shard_map/all_gather | solution.py:40
  120.2 0.0 copy-done.6
  120.2 5.1 multiply_reduce_fusion.3
  125.4 0.0 copy-done.4
  125.4 3.5 convolution_convert_fusion
  128.8 0.0 reduce-scatter.5.cloned.1.call-update
  128.8 0.0 reduce-scatter.7.cloned.1.call-start
  128.9 62.7 %psum.49 = f32[272]{0:T(512)S(1)} all-reduce(f32[272]{0:T(512)S(1)} %get-tuple-element.23), channel_id=1, replica_groups=mesh['dp'=4,'fsdp'=32] {'fsdp'}, use_global_device_ids=true, to_apply=%region_1.2 | all-reduce | flops 272 | bytes 2176 | tf_op jit(solution)/shard_map/psum | solution.py:45
  191.6 0.0 copy-done.8
  191.6 0.1 fusion.37
  191.7 0.1 pad_maximum_fusion.2
  191.7 18.3 %reduce-scatter.5.cloned.1.call-done = bf16[272,256]{1,0:T(8,128)(2,1)} async-done(((bf16[272,8192]{1,0:T(8,128)(2,1)}), bf16[272,256]{1,0:T(8,128)(2,1)}) %reduce-scatter.5.cloned.1.call-update) | async-done | bytes 139280 | tf_op jit(solution)/shard_map/reduce_scatter | solution.py:50
  210.1 0.0 copy-done.5
  210.1 1.0 convert_multiply_fusion.5
  211.0 4.2 convolution_convert_fusion.3
  215.3 0.0 reduce-scatter.7.cloned.1.call-update
  215.3 0.0 all-gather.9.cloned.1.call-start
  215.3 48.5 %reduce-scatter.7.cloned.1.call-done = bf16[2048,256]{1,0:T(8,128)(2,1)} async-done(((bf16[8192,256]{1,0:T(8,128)(2,1)}), bf16[2048,256]{1,0:T(8,128)(2,1)}) %reduce-scatter.7.cloned.1.call-update) | async-done | bytes 1048592 | tf_op jit(solution)/shard_map/reduce_scatter | solution.py:62
  263.8 0.0 all-gather.9.cloned.1.call-update
  263.9 0.0 copy-start.7
  263.9 0.0 reduce-scatter.9.cloned.1.call-start
  263.9 49.5 %all-gather.9.cloned.1.call-done = bf16[8192,256]{1,0:T(8,128)(2,1)} async-done(((bf16[2048,256]{1,0:T(8,128)(2,1)}), bf16[8192,256]{1,0:T(8,128)(2,1)}) %all-gather.9.cloned.1.call-update) | async-done | bytes 4194320 | tf_op jit(solution)/shard_map/all_gather | solution.py:70
  313.4 4.8 fusion.22
  318.2 62.7 %psum.51 = f32[256]{0:T(256)S(1)} all-reduce(f32[256]{0:T(256)S(1)} %fusion.22), channel_id=1, replica_groups=mesh['dp'=4,'fsdp'=32] {'fsdp'}, use_global_device_ids=true, to_apply=%region_7.8 | all-reduce | flops 256 | bytes 2048 | tf_op jit(solution)/shard_map/psum | solution.py:72
  380.9 0.0 copy-done.7
  380.9 5.5 convolution_convert_fusion.2
  386.4 0.0 reduce-scatter.9.cloned.1.call-update
  386.5 0.0 all-gather.11.cloned.1.call-start
  386.5 46.8 %reduce-scatter.9.cloned.1.call-done = bf16[2048,256]{1,0:T(8,128)(2,1)} async-done(((bf16[8192,256]{1,0:T(8,128)(2,1)}), bf16[2048,256]{1,0:T(8,128)(2,1)}) %reduce-scatter.9.cloned.1.call-update) | async-done | bytes 1048592 | tf_op jit(solution)/shard_map/reduce_scatter | solution.py:81
  433.3 0.0 copy-done.1
  433.3 2.5 fusion.8
  435.8 64.6 %all-reduce = (f32[]{:T(128)}, f32[]{:T(128)}) all-reduce(f32[]{:T(128)} %get-tuple-element.3, f32[]{:T(128)} %get-tuple-element.2), channel_id=1, replica_groups=mesh['dp'=4,'fsdp'=32] {'dp','fsdp'}, use_global_device_ids=true, to_apply=%region_5.6 | all-reduce | flops 2 | bytes 16 | tf_op jit(solution)/shard_map/psum | solution.py:18
  502.3 2.4 multiply_reduce_fusion.2
  504.7 64.3 %psum.53 = f32[]{:T(128)} all-reduce(f32[]{:T(128)} %multiply_reduce_fusion.2), channel_id=1, replica_groups=mesh['dp'=4,'fsdp'=32] {'dp','fsdp'}, use_global_device_ids=true, to_apply=%region_12.13 | all-reduce | flops 1 | bytes 8 | tf_op jit(solution)/shard_map/psum | solution.py:18
  570.4 0.0 copy-done.2
  570.4 2.3 multiply_reduce_fusion
  572.7 0.0 all-gather.11.cloned.1.call-update
  572.7 0.0 reduce-scatter.11.cloned.1.call-start
  572.7 45.0 %all-gather.11.cloned.1.call-done = bf16[8192,256]{1,0:T(8,128)(2,1)} async-done(((bf16[2048,256]{1,0:T(8,128)(2,1)}), bf16[8192,256]{1,0:T(8,128)(2,1)}) %all-gather.11.cloned.1.call-update) | async-done | bytes 4194320 | tf_op jit(solution)/shard_map/all_gather | solution.py:70
  617.7 4.8 fusion.19
  622.5 62.7 %psum.54 = f32[256]{0:T(256)S(1)} all-reduce(f32[256]{0:T(256)S(1)} %fusion.19), channel_id=1, replica_groups=mesh['dp'=4,'fsdp'=32] {'fsdp'}, use_global_device_ids=true, to_apply=%region_14.15 | all-reduce | flops 256 | bytes 2048 | tf_op jit(solution)/shard_map/psum | solution.py:72
  685.2 5.5 convolution_convert_fusion.1
  690.7 0.0 reduce-scatter.11.cloned.1.call-update
  691.5 46.1 %reduce-scatter.11.cloned.1.call-done = bf16[2048,256]{1,0:T(8,128)(2,1)} async-done(((bf16[8192,256]{1,0:T(8,128)(2,1)}), bf16[2048,256]{1,0:T(8,128)(2,1)}) %reduce-scatter.11.cloned.1.call-update) | async-done | bytes 1048592 | tf_op jit(solution)/shard_map/reduce_scatter | solution.py:94
  737.6 2.4 multiply_reduce_fusion.1
  740.6 64.5 %psum.55 = f32[]{:T(128)} all-reduce(f32[]{:T(128)S(6)} %add.83), channel_id=1, replica_groups=mesh['dp'=4,'fsdp'=32] {'dp','fsdp'}, use_global_device_ids=true, to_apply=%region_18.19 | all-reduce | flops 1 | bytes 8 | tf_op jit(solution)/shard_map/psum | solution.py:18
  806.5 0.5 add_multiply_fusion
  807.0 2.1 fusion.9
  (13 shorter events, 0.1 us)
Async XLA Ops:
  7.2 1.7 copy-start
  7.2 58.0 %all-gather.5.cloned.1.call-start = ((), (), s32[]{:S(2)}) async-start(), calls=%async_computation.4 | async-start | bytes 4595712 | tf_op jit(solution)/shard_map/all_gather | solution.py:35
  11.7 108.5 %copy-start.6 = (f32[256]{0:T(256)S(1)}, f32[256]{0:T(256)}, u32[]{:S(2)}) copy-start(f32[256]{0:T(256)} %param.15) | copy-start | bytes 3076
  11.7 108.5 %all-gather.7.cloned.1.call-start = ((), (), s32[]{:S(2)}) async-start(), calls=%async_computation.5 | async-start | bytes 4595712 | tf_op jit(solution)/shard_map/all_gather | solution.py:40
  70.8 139.3 %reduce-scatter.5.cloned.1.call-start = ((), (), s32[]{:S(2)}) async-start(), calls=%async_computation.6 | async-start | bytes 4595712 | tf_op jit(solution)/shard_map/reduce_scatter | solution.py:50
  120.2 5.1 copy-start.4
  128.8 62.8 %copy-start.8 = (s32[8]{0:T(128)S(1)}, s32[8]{0:T(128)}, u32[]{:S(2)}) copy-start(s32[8]{0:T(128)} %param.12) | copy-start | bytes 100
  128.8 81.3 %copy-start.5 = (bf16[272,256]{1,0:T(8,128)(2,1)S(1)}, bf16[272,256]{1,0:T(8,128)(2,1)}, u32[]{:S(2)}) copy-start(bf16[272,256]{1,0:T(8,128)(2,1)} %fusion.17) | copy-start | bytes 417796
  128.8 135.0 %reduce-scatter.7.cloned.1.call-start = ((), (), s32[]{:S(2)}) async-start(), calls=%async_computation.7 | async-start | bytes 5242880 | tf_op jit(solution)/shard_map/reduce_scatter | solution.py:62
  215.3 98.1 %all-gather.9.cloned.1.call-start = ((), (), s32[]{:S(2)}) async-start(), calls=%async_computation.8 | async-start | bytes 5242880 | tf_op jit(solution)/shard_map/all_gather | solution.py:70
  263.9 117.0 %copy-start.7 = (s32[128]{0:T(128)S(1)}, s32[128]{0:T(128)}, u32[]{:S(2)}) copy-start(s32[128]{0:T(128)} %param.10) | copy-start | bytes 1540
  263.9 169.4 %reduce-scatter.9.cloned.1.call-start = ((), (), s32[]{:S(2)}) async-start(), calls=%async_computation.9 | async-start | bytes 5242880 | tf_op jit(solution)/shard_map/reduce_scatter | solution.py:81
  386.4 46.9 %copy-start.1 = (bf16[2048,256]{1,0:T(8,128)(2,1)S(1)}, bf16[2048,256]{1,0:T(8,128)(2,1)}, u32[]{:S(2)}) copy-start(bf16[2048,256]{1,0:T(8,128)(2,1)} %reduce-scatter.7.cloned.1.call-done) | copy-start | bytes 3145732
  386.5 231.2 %all-gather.11.cloned.1.call-start = ((), (), s32[]{:S(2)}) async-start(), calls=%async_computation.10 | async-start | bytes 5242880 | tf_op jit(solution)/shard_map/all_gather | solution.py:70
  433.3 137.1 %copy-start.2 = (bf16[2048,256]{1,0:T(8,128)(2,1)S(1)}, bf16[2048,256]{1,0:T(8,128)(2,1)}, u32[]{:S(2)}) copy-start(bf16[2048,256]{1,0:T(8,128)(2,1)} %reduce-scatter.9.cloned.1.call-done) | copy-start | bytes 3145732
  572.7 164.9 %reduce-scatter.11.cloned.1.call-start = ((), (), s32[]{:S(2)}) async-start(), calls=%async_computation.11 | async-start | bytes 5242880 | tf_op jit(solution)/shard_map/reduce_scatter | solution.py:94
  690.7 46.9 %copy-start.3 = (bf16[2048,256]{1,0:T(8,128)(2,1)S(1)}, bf16[2048,256]{1,0:T(8,128)(2,1)}, u32[]{:S(2)}) copy-start(bf16[2048,256]{1,0:T(8,128)(2,1)} %get-tuple-element.12) | copy-start | bytes 3145732
Sparse Core Ops, SparseCore 0:
  11.8 53.3 all-gather.4
  70.9 49.2 all-gather.6
  129.0 81.0 reduce-scatter.4
  215.4 48.3 reduce-scatter.6
  265.4 47.9 all-gather.8
  386.6 46.6 reduce-scatter.8
  572.8 44.8 all-gather.10
  690.9 46.6 reduce-scatter.10
where the time goes:
time: 817 us; the launch traced here: 816 us
  blocking collectives  381 us (47%)
  waiting for transfers between devices  357 us (44%)
  matrix products  38.9 us (5%)
  between operations  20.2 us (2%)
  other arithmetic  14.2 us (2%)
    psum x3, blocking collectives, solver_total(): return lax.psum(value, ('dp', 'fsdp'))  193 us
    psum x2, blocking collectives, apply_curvature(): response = lax.psum(jnp.sum(train_mix * project, axis=1), 'fsdp')  125 us
    all_gather x2, waiting for transfers between devices, apply_curvature(): gathered = lax.all_gather(packed, 'dp', axis=0, tiled=True)  94.4 us
    psum x1, blocking collectives, local(): scores_all = lax.psum(jnp.sum(output_act * head_weight, axis=1), 'fsdp')  62.7 us
    all_gather x1, waiting for transfers between devices, local(): feats = lax.all_gather(local_rows, 'fsdp', axis=1, tiled=True)  53.5 us
    all_gather x1, waiting for transfers between devices, local(): lax.all_gather(hidden, 'fsdp', axis=1, tiled=True)  49.4 us
    reduce_scatter x1, waiting for transfers between devices, local(): lax.psum_scatter(grad_local.astype(jnp.bfloat16), 'dp', scatter_dimension...  48.5 us
    reduce_scatter x1, waiting for transfers between devices, local(): lax.psum_scatter(local_first.astype(jnp.bfloat16), 'dp', scatter_dimensio...  46.8 us
  transfers between devices with their start and end apart: 8, of which 8 were waited for; matrix products, arithmetic and copies ran while one was open for 0% of the time, Pallas kernels for 0%

commit v1 on v0

--- a/solution.py
+++ b/solution.py
@@ -67,7 +67,16 @@
 
     def apply_curvature(direction):
         packed = direction.astype(jnp.bfloat16)
-        gathered = lax.all_gather(packed, "dp", axis=0, tiled=True)
+        ways = lax.axis_size("dp")
+        up = [(d, (d + 1) % ways) for d in range(ways)]
+        down = [(d, (d - 1) % ways) for d in range(ways)]
+        earlier, later = ([packed], [packed])
+        for _ in range(ways // 2):
+            earlier.append(lax.ppermute(earlier[-1], "dp", up))
+        for _ in range((ways - 1) // 2):
+            later.append(lax.ppermute(later[-1], "dp", down))
+        line = jnp.concatenate([*earlier[::-1], *later[1:]], axis=0)
+        gathered = jnp.roll(line, (lax.axis_index("dp") - ways // 2) * packed.shape[0], axis=0)
         project = jnp.dot(train_feats, gathered, preferred_element_type=jnp.float32)
         response = lax.psum(jnp.sum(train_mix * project, axis=1), "fsdp")
         rdiff = response[:npairs] - response[npairs:]

time: 817 us -> 871 us (1.066)
  matrix products: 38.9 us -> 88.7 us
  waiting for transfers between devices: 357 us -> 347 us
    all_gather x2 -> x0, waiting for transfers between devices: 94.4 us -> none  [apply_curvature(): gathered = lax.all_gather(packed, 'dp', axis=0, tiled=True)]
    ppermute x0 -> x6, waiting for transfers between devices: none -> 93.7 us  [the longest x4 93.7 us: apply_curvature(): earlier.append(lax.ppermute(earlier[-1], 'dp', up))]
    dot_general x2, matrix products: 9.58 us -> 59.3 us  [apply_curvature(): project = jnp.dot(train_feats, gathered, preferred_element_type=jnp.float32)]
  transfers between devices with their start and end apart: 8 -> 12, of which waited for: 8 -> 10; matrix products, arithmetic and copies ran while one was open for 0% -> 0% of each run, Pallas kernels for 0% -> 0%
where the time goes in v1:
time: 871 us; the launch traced here: 865 us
  blocking collectives  386 us (44%)
  waiting for transfers between devices  347 us (40%)
  matrix products  88.7 us (10%)
  between operations  20.5 us (2%)
  other arithmetic  13.2 us (2%)
    psum x3, blocking collectives, solver_total(): return lax.psum(value, ('dp', 'fsdp'))  193 us
    psum x2, blocking collectives, apply_curvature(): response = lax.psum(jnp.sum(train_mix * project, axis=1), 'fsdp')  130 us
    ppermute x4, waiting for transfers between devices, apply_curvature(): earlier.append(lax.ppermute(earlier[-1], 'dp', up))  93.7 us
    psum x1, blocking collectives, local(): scores_all = lax.psum(jnp.sum(output_act * head_weight, axis=1), 'fsdp')  62.7 us
    dot_general x2, matrix products, apply_curvature(): project = jnp.dot(train_feats, gathered, preferred_element_type=jnp.float32)  59.3 us
    all_gather x1, waiting for transfers between devices, local(): feats = lax.all_gather(local_rows, 'fsdp', axis=1, tiled=True)  53.5 us
    all_gather x1, waiting for transfers between devices, local(): lax.all_gather(hidden, 'fsdp', axis=1, tiled=True)  49.4 us
    reduce_scatter x1, waiting for transfers between devices, local(): lax.psum_scatter(grad_local.astype(jnp.bfloat16), 'dp', scatter_dimension...  48.5 us
  transfers between devices with their start and end apart: 12, of which 10 were waited for; matrix products, arithmetic and copies ran while one was open for 0% of the time, Pallas kernels for 0%

profile of v1, /device:TPU:1, one launch (start us, length us, event | category | flops | bytes accessed | tf_op | source)
XLA Modules:
  0.0 864.7 jit_solution(5373859666927964667)
XLA Ops:
  7.2 0.0 copy-start
  7.2 0.0 all-gather.3.cloned.1.call-start
  7.2 0.8 slice_bitcast_fusion.3
  8.0 0.8 slice_bitcast_fusion.1
  8.7 0.1 fusion.59
  8.8 0.0 copy-done
  8.8 2.0 gather_fusion
  10.8 0.1 compare_and_fusion
  10.9 0.8 broadcast_select_fusion
  11.7 0.0 all-gather.3.cloned.1.call-update
  11.7 0.0 copy-start.6
  11.7 0.0 all-gather.5.cloned.1.call-start
  11.8 53.5 %all-gather.3.cloned.1.call-done = bf16[272,8192]{1,0:T(8,128)(2,1)} async-done(((bf16[272,256]{1,0:T(8,128)(2,1)}), bf16[272,8192]{1,0:T(8,128)(2,1)}) %all-gather.3.cloned.1.call-update) | async-done | bytes 4456464 | tf_op jit(solution)/shard_map/all_gather | solution.py:35
  65.2 5.5 fusion.37
  70.8 0.0 all-gather.5.cloned.1.call-update
  70.8 0.0 reduce-scatter.5.cloned.1.call-start
  70.8 49.4 %all-gather.5.cloned.1.call-done = bf16[272,8192]{1,0:T(8,128)(2,1)} async-done(((bf16[272,256]{1,0:T(8,128)(2,1)}), bf16[272,8192]{1,0:T(8,128)(2,1)}) %all-gather.5.cloned.1.call-update) | async-done | bytes 4456464 | tf_op jit(solution)/shard_map/all_gather | solution.py:40
  120.2 5.1 multiply_reduce_fusion.3
  125.4 3.5 convolution_convert_fusion
  128.8 0.0 reduce-scatter.5.cloned.1.call-update
  128.9 0.0 reduce-scatter.7.cloned.1.call-start
  128.9 62.7 %psum.49 = f32[272]{0:T(512)S(1)} all-reduce(f32[272]{0:T(512)S(1)} %get-tuple-element.24), channel_id=1, replica_groups=mesh['dp'=4,'fsdp'=32] {'fsdp'}, use_global_device_ids=true, to_apply=%region_1.2 | all-reduce | flops 272 | bytes 2176 | tf_op jit(solution)/shard_map/psum | solution.py:45
  191.6 0.1 fusion.65
  191.7 0.1 pad_maximum_fusion.2
  191.7 18.3 %reduce-scatter.5.cloned.1.call-done = bf16[272,256]{1,0:T(8,128)(2,1)} async-done(((bf16[272,8192]{1,0:T(8,128)(2,1)}), bf16[272,256]{1,0:T(8,128)(2,1)}) %reduce-scatter.5.cloned.1.call-update) | async-done | bytes 139280 | tf_op jit(solution)/shard_map/reduce_scatter | solution.py:50
  210.1 1.0 convert_multiply_fusion.5
  211.0 0.0 copy-start.5
  211.0 4.3 convolution_convert_fusion.3
  215.4 0.0 reduce-scatter.7.cloned.1.call-update
  215.4 0.0 reduce-scatter.9.cloned.1.call-start
  215.4 48.5 %reduce-scatter.7.cloned.1.call-done = bf16[2048,256]{1,0:T(8,128)(2,1)} async-done(((bf16[8192,256]{1,0:T(8,128)(2,1)}), bf16[2048,256]{1,0:T(8,128)(2,1)}) %reduce-scatter.7.cloned.1.call-update) | async-done | bytes 1048592 | tf_op jit(solution)/shard_map/reduce_scatter | solution.py:62
  263.9 0.0 collective-permute-start
  264.0 2.7 collective-permute-start.2
  266.6 22.8 %collective-permute-done = bf16[2048,256]{1,0:T(8,128)(2,1)S(1)} collective-permute-done((bf16[2048,256]{1,0:T(8,128)(2,1)}, bf16[2048,256]{1,0:T(8,128)(2,1)S(1)}, u32[]{:S(2)}, u32[]{:S(2)}) %collective-permute-start) | collective-permute-done | bytes 1048608 | tf_op jit(solution)/shard_map/ppermute | solution.py:75
  289.4 0.3 collective-permute-start.1
  289.7 0.0 copy-start.7
  289.8 0.0 collective-permute-done.2
  289.8 24.4 %collective-permute-done.1 = bf16[2048,256]{1,0:T(8,128)(2,1)} collective-permute-done((bf16[2048,256]{1,0:T(8,128)(2,1)S(1)}, bf16[2048,256]{1,0:T(8,128)(2,1)}, u32[]{:S(2)}, u32[]{:S(2)}) %collective-permute-start.1) | collective-permute-done | bytes 1048608 | tf_op jit(solution)/shard_map/ppermute | solution.py:75
  314.2 23.2 %fusion.39 = f32[256]{0:T(256)S(1)} fusion(s32[]{:T(128)S(6)} %select_n.36, bf16[2048,256]{1,0:T(8,128)(2,1)} %collective-permute-done.1, bf16[2048,256]{1,0:T(8,128)(2,1)S(1)} %collective-permute-done, bf16[2048,256]{1,0:T(8,128)(2,1)} %reduce-scatter.7.cloned.1.call-done, bf16[2048,256]{1,0:T(8,128)(2,1)S(1)} %collective-permute-done.2, ...), kind=kOutput, calls=%fused_computation.62 | convolution fusion | flops 1107427072 | bytes 8651780 | tf_op jit(solution)/shard_map/dot_general | solution.py:80
  337.4 65.0 %psum.51 = f32[256]{0:T(256)S(1)} all-reduce(f32[256]{0:T(256)S(1)} %fusion.39), channel_id=1, replica_groups=mesh['dp'=4,'fsdp'=32] {'fsdp'}, use_global_device_ids=true, to_apply=%region_7.9 | all-reduce | flops 256 | bytes 2048 | tf_op jit(solution)/shard_map/psum | solution.py:81
  402.4 5.5 convolution_convert_fusion.2
  407.9 0.0 reduce-scatter.9.cloned.1.call-update
  408.0 0.0 reduce-scatter.11.cloned.1.call-start
  408.0 43.1 %reduce-scatter.9.cloned.1.call-done = bf16[2048,256]{1,0:T(8,128)(2,1)} async-done(((bf16[8192,256]{1,0:T(8,128)(2,1)}), bf16[2048,256]{1,0:T(8,128)(2,1)}) %reduce-scatter.9.cloned.1.call-update) | async-done | bytes 1048592 | tf_op jit(solution)/shard_map/reduce_scatter | solution.py:90
  451.1 2.5 fusion.24
  453.6 64.6 %all-reduce = (f32[]{:T(128)}, f32[]{:T(128)}) all-reduce(f32[]{:T(128)} %get-tuple-element.4, f32[]{:T(128)} %get-tuple-element.3), channel_id=1, replica_groups=mesh['dp'=4,'fsdp'=32] {'dp','fsdp'}, use_global_device_ids=true, to_apply=%region_5.6 | all-reduce | flops 2 | bytes 16 | tf_op jit(solution)/shard_map/psum | solution.py:18
  520.2 2.4 multiply_reduce_fusion.2
  522.6 64.1 %psum.53 = f32[]{:T(128)} all-reduce(f32[]{:T(128)} %multiply_reduce_fusion.2), channel_id=1, replica_groups=mesh['dp'=4,'fsdp'=32] {'dp','fsdp'}, use_global_device_ids=true, to_apply=%region_12.14 | all-reduce | flops 1 | bytes 8 | tf_op jit(solution)/shard_map/psum | solution.py:18
  588.1 1.3 multiply_reduce_fusion
  589.4 0.0 collective-permute-start.3
  589.4 2.7 collective-permute-start.5
  592.1 22.4 %collective-permute-done.3 = bf16[2048,256]{1,0:T(8,128)(2,1)S(1)} collective-permute-done((bf16[2048,256]{1,0:T(8,128)(2,1)S(1)}, bf16[2048,256]{1,0:T(8,128)(2,1)S(1)}, u32[]{:S(2)}, u32[]{:S(2)}) %collective-permute-start.3) | collective-permute-done | bytes 1048608 | tf_op jit(solution)/shard_map/ppermute | solution.py:75
  614.5 0.2 collective-permute-start.4
  614.6 0.0 collective-permute-done.5
  614.7 24.1 %collective-permute-done.4 = bf16[2048,256]{1,0:T(8,128)(2,1)S(1)} collective-permute-done((bf16[2048,256]{1,0:T(8,128)(2,1)S(1)}, bf16[2048,256]{1,0:T(8,128)(2,1)S(1)}, u32[]{:S(2)}, u32[]{:S(2)}) %collective-permute-start.4) | collective-permute-done | bytes 1048608 | tf_op jit(solution)/shard_map/ppermute | solution.py:75
  638.8 36.1 %fusion.44 = f32[256]{0:T(256)S(1)} fusion(s32[]{:T(128)S(6)} %select_n.36, bf16[2048,256]{1,0:T(8,128)(2,1)S(1)} %collective-permute-done.4, bf16[2048,256]{1,0:T(8,128)(2,1)S(1)} %collective-permute-done.3, bf16[2048,256]{1,0:T(8,128)(2,1)S(1)} %get-tuple-element.13, bf16[2048,256]{1,0:T(8,128)(2,1)S(1)} %collective-permute-done.5, ...), kind=kOutput, calls=%fused_computation.63 | convolution fusion | flops 1107427072 | bytes 8651780 | tf_op jit(solution)/shard_map/dot_general | solution.py:80
  674.8 64.8 %psum.54 = f32[256]{0:T(256)S(1)} all-reduce(f32[256]{0:T(256)S(1)} %fusion.44), channel_id=1, replica_groups=mesh['dp'=4,'fsdp'=32] {'fsdp'}, use_global_device_ids=true, to_apply=%region_14.16 | all-reduce | flops 256 | bytes 2048 | tf_op jit(solution)/shard_map/psum | solution.py:81
  739.7 5.5 convolution_convert_fusion.1
  745.2 0.0 reduce-scatter.11.cloned.1.call-update
  745.9 40.3 %reduce-scatter.11.cloned.1.call-done = bf16[2048,256]{1,0:T(8,128)(2,1)} async-done(((bf16[8192,256]{1,0:T(8,128)(2,1)}), bf16[2048,256]{1,0:T(8,128)(2,1)}) %reduce-scatter.11.cloned.1.call-update) | async-done | bytes 1048592 | tf_op jit(solution)/shard_map/reduce_scatter | solution.py:103
  786.2 2.4 multiply_reduce_fusion.1
  789.2 64.5 %psum.55 = f32[]{:T(128)} all-reduce(f32[]{:T(128)S(6)} %add.92), channel_id=1, replica_groups=mesh['dp'=4,'fsdp'=32] {'dp','fsdp'}, use_global_device_ids=true, to_apply=%region_18.20 | all-reduce | flops 1 | bytes 8 | tf_op jit(solution)/shard_map/psum | solution.py:18
  855.0 0.5 add_multiply_fusion
  855.6 2.1 fusion.25
  (19 shorter events, 0.1 us)
Async XLA Ops:
  7.2 1.7 copy-start
  7.2 58.0 %all-gather.3.cloned.1.call-start = ((), (), s32[]{:S(2)}) async-start(), calls=%async_computation.4 | async-start | bytes 4595712 | tf_op jit(solution)/shard_map/all_gather | solution.py:35
  11.7 108.5 %copy-start.6 = (f32[256]{0:T(256)S(1)}, f32[256]{0:T(256)}, u32[]{:S(2)}) copy-start(f32[256]{0:T(256)} %param.17) | copy-start | bytes 3076
  11.7 108.5 %all-gather.5.cloned.1.call-start = ((), (), s32[]{:S(2)}) async-start(), calls=%async_computation.5 | async-start | bytes 4595712 | tf_op jit(solution)/shard_map/all_gather | solution.py:40
  70.8 139.3 %reduce-scatter.5.cloned.1.call-start = ((), (), s32[]{:S(2)}) async-start(), calls=%async_computation.6 | async-start | bytes 4595712 | tf_op jit(solution)/shard_map/reduce_scatter | solution.py:50
  120.2 5.1 copy-start.3
  128.8 62.8 %copy-start.8 = (s32[8]{0:T(128)S(1)}, s32[8]{0:T(128)}, u32[]{:S(2)}) copy-start(s32[8]{0:T(128)} %param.14) | copy-start | bytes 100
  128.8 81.3 %copy-start.4 = (bf16[272,256]{1,0:T(8,128)(2,1)S(1)}, bf16[272,256]{1,0:T(8,128)(2,1)}, u32[]{:S(2)}) copy-start(bf16[272,256]{1,0:T(8,128)(2,1)} %fusion.37) | copy-start | bytes 417796
  128.9 135.1 %reduce-scatter.7.cloned.1.call-start = ((), (), s32[]{:S(2)}) async-start(), calls=%async_computation.7 | async-start | bytes 5242880 | tf_op jit(solution)/shard_map/reduce_scatter | solution.py:62
  211.0 191.4 %copy-start.5 = (f32[272,256]{1,0:T(8,128)}, f32[272,256]{1,0:T(8,128)S(1)}, u32[]{:S(2)}) copy-start(f32[272,256]{1,0:T(8,128)S(1)} %convert_multiply_fusion.5) | copy-start | bytes 835588
  215.4 235.7 %reduce-scatter.9.cloned.1.call-start = ((), (), s32[]{:S(2)}) async-start(), calls=%async_computation.8 | async-start | bytes 5242880 | tf_op jit(solution)/shard_map/reduce_scatter | solution.py:90
  263.9 25.5 %collective-permute-start = (bf16[2048,256]{1,0:T(8,128)(2,1)}, bf16[2048,256]{1,0:T(8,128)(2,1)S(1)}, u32[]{:S(2)}, u32[]{:S(2)}) collective-permute-start(bf16[2048,256]{1,0:T(8,128)(2,1)} %reduce-scatter.7.cloned.1.call-done), channel_id=1, source_target_pairs={{0,32},{32,64},{64,96},{96,0},{1,33},{33,65},{65,97},{97,1},{2,34}... | collective-permute-start | bytes 3145736 | tf_op jit(solution)/shard_map/ppermute | solution.py:75
  264.0 25.8 %collective-permute-start.2 = (bf16[2048,256]{1,0:T(8,128)(2,1)}, bf16[2048,256]{1,0:T(8,128)(2,1)S(1)}, u32[]{:S(2)}, u32[]{:S(2)}) collective-permute-start(bf16[2048,256]{1,0:T(8,128)(2,1)} %reduce-scatter.7.cloned.1.call-done), channel_id=1, source_target_pairs={{0,96},{32,0},{64,32},{96,64},{1,97},{33,1},{65,33},{97,65},{2,98}... | collective-permute-start | bytes 3145736 | tf_op jit(solution)/shard_map/ppermute | solution.py:77
  289.4 24.7 %collective-permute-start.1 = (bf16[2048,256]{1,0:T(8,128)(2,1)S(1)}, bf16[2048,256]{1,0:T(8,128)(2,1)}, u32[]{:S(2)}, u32[]{:S(2)}) collective-permute-start(bf16[2048,256]{1,0:T(8,128)(2,1)S(1)} %collective-permute-done), channel_id=1, source_target_pairs={{0,32},{32,64},{64,96},{96,0},{1,33},{33,65},{65,97},{97,1},{2,34}... | collective-permute-start | bytes 3145736 | tf_op jit(solution)/shard_map/ppermute | solution.py:75
  289.7 112.6 %copy-start.7 = (s32[128]{0:T(128)S(1)}, s32[128]{0:T(128)}, u32[]{:S(2)}) copy-start(s32[128]{0:T(128)} %param.12) | copy-start | bytes 1540
  407.9 43.2 %copy-start.1 = (bf16[2048,256]{1,0:T(8,128)(2,1)S(1)}, bf16[2048,256]{1,0:T(8,128)(2,1)}, u32[]{:S(2)}) copy-start(bf16[2048,256]{1,0:T(8,128)(2,1)} %reduce-scatter.7.cloned.1.call-done) | copy-start | bytes 3145732
  408.0 378.2 %reduce-scatter.11.cloned.1.call-start = ((), (), s32[]{:S(2)}) async-start(), calls=%async_computation.9 | async-start | bytes 5242880 | tf_op jit(solution)/shard_map/reduce_scatter | solution.py:103
  451.1 137.0 %copy-start.2 = (bf16[2048,256]{1,0:T(8,128)(2,1)S(1)}, bf16[2048,256]{1,0:T(8,128)(2,1)}, u32[]{:S(2)}) copy-start(bf16[2048,256]{1,0:T(8,128)(2,1)} %reduce-scatter.9.cloned.1.call-done) | copy-start | bytes 3145732
  589.4 25.1 %collective-permute-start.3 = (bf16[2048,256]{1,0:T(8,128)(2,1)S(1)}, bf16[2048,256]{1,0:T(8,128)(2,1)S(1)}, u32[]{:S(2)}, u32[]{:S(2)}) collective-permute-start(bf16[2048,256]{1,0:T(8,128)(2,1)S(1)} %get-tuple-element.13), channel_id=1, source_target_pairs={{0,32},{32,64},{64,96},{96,0},{1,33},{33,65},{65,97},{97,1},{2,34}... | collective-permute-start | bytes 3145736 | tf_op jit(solution)/shard_map/ppermute | solution.py:75
  589.4 25.2 %collective-permute-start.5 = (bf16[2048,256]{1,0:T(8,128)(2,1)S(1)}, bf16[2048,256]{1,0:T(8,128)(2,1)S(1)}, u32[]{:S(2)}, u32[]{:S(2)}) collective-permute-start(bf16[2048,256]{1,0:T(8,128)(2,1)S(1)} %get-tuple-element.13), channel_id=1, source_target_pairs={{0,96},{32,0},{64,32},{96,64},{1,97},{33,1},{65,33},{97,65},{2,98}... | collective-permute-start | bytes 3145736 | tf_op jit(solution)/shard_map/ppermute | solution.py:77
  614.5 24.3 %collective-permute-start.4 = (bf16[2048,256]{1,0:T(8,128)(2,1)S(1)}, bf16[2048,256]{1,0:T(8,128)(2,1)S(1)}, u32[]{:S(2)}, u32[]{:S(2)}) collective-permute-start(bf16[2048,256]{1,0:T(8,128)(2,1)S(1)} %collective-permute-done.3), channel_id=1, source_target_pairs={{0,32},{32,64},{64,96},{96,0},{1,33},{33,65},{65,97},{97,1},{2,34}... | collective-permute-start | bytes 3145736 | tf_op jit(solution)/shard_map/ppermute | solution.py:75
Sparse Core Ops, SparseCore 0:
  11.8 53.3 all-gather.2
  70.9 49.2 all-gather.4
  129.0 81.0 reduce-scatter.4
  215.5 48.3 reduce-scatter.6
  408.1 42.9 reduce-scatter.8
  745.4 40.7 reduce-scatter.10
